TPU v7x, 32 devices: a whole 2x2x4 slice. The times are simulated.
32 devices in a mesh: field: 16 (over z, y, core), probe: 2 (over x).
Axes of the slice: x: 2, y: 2, z: 4, core: 2. Of those that a mesh axis runs over, the one named last changes fastest.
Arguments:
- probes: bfloat16 [16, 4, 512, 256], P('probe', None, 'field'), may hold values from -6 to 6
- matern_shift: float32 [4, 512, 256], P(None, 'field'), may hold values from 0.25 to 2
- diffusivity: float32 [4, 512, 256], P(None, 'field'), may hold values from 0.03 to 0.1
- sensor_count: int32 [16], P('field'), may hold values from 1 to 256, 2560 in all
- sensor_cell: int32 [16, 256], P('field'), may hold values from 0 to 32767
- sensor_owner: int32 [16, 256, 1], P('field'), may hold values from 0 to 15; in each aligned block of 256 rows (0 to 255, 256 to 511, ..., all dimensions but the last counted through in order) at most 24 rows name the same one
- design_logit: float32 [16, 16, 24], P('field'), may hold values from -6 to 6
- noise_precision: float32 [16, 16, 24], P('field'), may hold values from 1 to 8
Outputs:
- hessian_probes: float32 [16, 4, 512, 256], P('probe', None, 'field')
- tiles: float32 [16, 16], P('probe')
- weight_grad: float32 [16, 16, 24], P('field')
Inputs may be any that keep to these rules, and one draw needn't show every extreme that they name: `sensor_count`: the counts sum to 2560 and the largest is 256. `sensor_cell`: flat cell index within the block; several slots may share a cell. `sensor_owner`: among the 256 slots of one block, live or not, no owner is named by more than 24 slots, a bound that some block reaches.
All inputs are finite; a program needn't handle non-finite values. No bound on the sum of `sensor_count` on one device may be relied on, other than what follows from the above.
Results may differ from a plain program's by a relative error of at most 0.00035.
Values may be sent and summed in bfloat16 or wider, within the bound.
A program may use at most 128 MiB of HBM per device.

v0:
```python
import math

import jax
import jax.numpy as jnp
from jax import lax
from jax.sharding import PartitionSpec as P

SWEEPS = 4
STEPS = 6
SENS_DEV = 160


advect_speed = 0.3


def with_halo(value, sides, width):
    for axis, dim in sides:
        size, length = (lax.axis_size(axis), value.shape[dim])
        up = [(i, (i + 1) % size) for i in range(size)]
        down = [(j, i) for i, j in up]
        last = lax.slice_in_dim(value, length - width, length, axis=dim)
        first = lax.slice_in_dim(value, 0, width, axis=dim)
        before = lax.ppermute(last, axis, up)
        after = lax.ppermute(first, axis, down)
        value = jnp.concatenate([before, value, after], axis=dim)
    return value


def neighbours(extended):
    middle = extended[:, :, 1:-1]
    west_cells = extended[:, :, :-2]
    east_cells = extended[:, :, 2:]
    side_pad = jnp.pad(middle, ((0, 0), (0, 0), (0, 0), (1, 1)))
    depth_pad = jnp.pad(middle, ((0, 0), (1, 1), (0, 0), (0, 0)))
    beside_all = (
        west_cells
        + east_cells
        + (side_pad[..., :-2] + side_pad[..., 2:])
        + (depth_pad[:, :-2] + depth_pad[:, 2:])
    )
    return (middle, west_cells, east_cells, beside_all)


def prior_apply(source, diagonal):
    state = source / diagonal
    for sweep in range(SWEEPS):
        extended = with_halo(state, (("field", 2),), 1)
        middle, west_cells, east_cells, beside_all = neighbours(extended)
        state = (source + beside_all) / diagonal
    return state


def on_device(
    probes,
    matern_shift,
    diffusivity,
    sensor_count,
    sensor_cell,
    sensor_owner,
    design_logit,
    noise_precision,
):
    probe_count = probes.shape[0]
    block_cx = probes.shape[2]
    cell_count = probes.shape[1] * probes.shape[2] * probes.shape[3]
    field_count = lax.axis_size("field")
    slot_cap = design_logit.shape[2]
    slot_count = sensor_cell.shape[1]
    diagonal = matern_shift + 6.0
    depth = 2
    coef_wide = with_halo(diffusivity, (("field", 1),), depth)
    state = prior_apply(probes.astype(jnp.float32), diagonal)
    for rounds in range(STEPS // depth):
        extended = with_halo(state, (("field", 2),), depth)
        for inner in range(depth):
            width = block_cx + 2 * (depth - inner - 1)
            coef_mid = coef_wide[:, inner + 1 : inner + 1 + width]
            middle, west_cells, east_cells, beside_all = neighbours(extended)
            extended = (
                middle
                + coef_mid * (beside_all - 6.0 * middle)
                - advect_speed * (middle - west_cells)
            )
        state = extended
    slots = jnp.arange(slot_count, dtype=jnp.int32)
    live = (slots < sensor_count[0]).astype(jnp.float32)
    cells = sensor_cell[0]
    owner = sensor_owner[0, :, 0]
    same = owner[:, None] == owner[None, :]
    earlier = slots[None, :] < slots[:, None]
    position = jnp.sum(jnp.logical_and(same, earlier), axis=1)
    target = owner * slot_cap + position
    table = (
        jnp.arange(field_count * slot_cap, dtype=jnp.int32)[:, None] == target[None, :]
    ).astype(jnp.float32)
    flat_state = state.reshape(probe_count, cell_count)
    observed = jnp.take(flat_state, cells, axis=1) * live[None, :]
    outgoing = lax.dot_general(
        table, observed, (((1,), (1,)), ((), ())), precision=lax.Precision.HIGHEST
    )
    outgoing = outgoing.reshape(field_count, slot_cap, probe_count)
    received = lax.all_to_all(outgoing, "field", split_axis=0, concat_axis=0, tiled=True)
    gated = jax.nn.sigmoid(design_logit[0])
    weight_slot = gated * noise_precision[0]
    weighted = received * weight_slot[:, :, None]
    returned = lax.all_to_all(weighted, "field", split_axis=0, concat_axis=0, tiled=True)
    per_sensor = lax.dot_general(
        table,
        returned.reshape(field_count * slot_cap, probe_count),
        (((0,), (0,)), ((), ())),
        precision=lax.Precision.HIGHEST,
    )
    injected = jnp.zeros((probe_count, cell_count), jnp.float32).at[:, cells].add(per_sensor.T)
    adjoint = injected.reshape(probes.shape)
    for rounds in range(STEPS // depth):
        extended = with_halo(adjoint, (("field", 2),), depth)
        for inner in range(depth):
            width = block_cx + 2 * (depth - inner)
            scaled = coef_wide[:, inner : inner + width] * extended
            scaled_mid, scaled_west, scaled_east, scaled_around = neighbours(scaled)
            middle = extended[:, :, 1:-1]
            east_cells = extended[:, :, 2:]
            extended = (
                middle + (scaled_around - 6.0 * scaled_mid) - advect_speed * (middle - east_cells)
            )
        adjoint = extended
    hessian_probes = prior_apply(adjoint, diagonal)
    flat_result = hessian_probes.reshape(probe_count, cell_count)
    piece = lax.all_gather(probes, "probe", axis=0, tiled=True)
    flat_piece = piece.reshape(piece.shape[0], cell_count).astype(jnp.float32)
    columns = lax.dot_general(
        flat_result, flat_piece, (((1,), (1,)), ((), ())), precision=lax.Precision.HIGHEST
    )
    scale_factor = 1.0 / math.sqrt(SENS_DEV * field_count)
    tiles = lax.psum(columns, "field") * scale_factor
    squares = jnp.sum(received * received, axis=2)
    total_squares = lax.psum(squares, "probe")
    weight_grad = gated * (1.0 - gated) * noise_precision[0] * total_squares
    return (hessian_probes, tiles, weight_grad[None])


def solution(mesh):
    in_specs = (
        P("probe", None, "field", None),
        P(None, "field", None),
        P(None, "field", None),
        P("field"),
        P("field", None),
        P("field", None, None),
        P("field", None, None),
        P("field", None, None),
    )
    out_specs = (P("probe", None, "field", None), P("probe", None), P("field", None, None))
    return jax.shard_map(
        on_device, mesh=mesh, in_specs=in_specs, out_specs=out_specs, check_vma=False
    )
```

profile of v0, /device:TPU:1, one launch (start us, length us, event | category | flops | bytes accessed | tf_op | source)
XLA Modules:
  0.0 231.3 jit_solution(16700310639509512461)
XLA Ops:
  7.2 1.0 broadcast_add_fusion
  8.2 1.2 convert_divide_fusion
  9.4 2.7 %collective-permute-start = (f32[8,4,1,256]{3,2,1,0:T(1,128)S(1)}, f32[8,4,1,256]{3,2,1,0:T(1,128)S(1)}, u32[]{:S(2)}, u32[]{:S(2)}) collective-permute-start(f32[8,4,1,256]{3,2,1,0:T(1,128)S(1)} %get-tuple-element.43), channel_id=1, source_target_pairs={{0,2},{2,4},{4,6},{6,8},{8,10},{10,12},{12,14},{14,16},{16,18},{18... | collective-permute-start | bytes 98312 | tf_op jit(solution)/shard_map/ppermute | solution.py:23
  12.1 1.8 collective-permute-start.10
  13.9 1.3 collective-permute-start.11
  15.7 0.7 fusion.135
  16.6 3.9 %collective-permute-start.3 = (f32[8,4,1,256]{3,2,1,0:T(1,128)S(1)}, f32[8,4,1,256]{3,2,1,0:T(1,128)S(1)}, u32[]{:S(2)}, u32[]{:S(2)}) collective-permute-start(f32[8,4,1,256]{3,2,1,0:T(1,128)S(1)} %get-tuple-element.42), channel_id=1, source_target_pairs={{2,0},{4,2},{6,4},{8,6},{10,8},{12,10},{14,12},{16,14},{18,16},{20... | collective-permute-start | bytes 98312 | tf_op jit(solution)/shard_map/ppermute | solution.py:24
  21.3 0.7 fusion.136
  22.1 5.2 %collective-permute-start.5 = (f32[8,4,1,256]{3,2,1,0:T(1,128)S(1)}, f32[8,4,1,256]{3,2,1,0:T(1,128)S(1)}, u32[]{:S(2)}, u32[]{:S(2)}) collective-permute-start(f32[8,4,1,256]{3,2,1,0:T(1,128)S(1)} %get-tuple-element.40), channel_id=1, source_target_pairs={{2,0},{4,2},{6,4},{8,6},{10,8},{12,10},{14,12},{16,14},{18,16},{20... | collective-permute-start | bytes 98312 | tf_op jit(solution)/shard_map/ppermute | solution.py:24
  28.2 0.7 fusion.137
  29.0 5.3 %collective-permute-start.7 = (f32[8,4,1,256]{3,2,1,0:T(1,128)S(1)}, f32[8,4,1,256]{3,2,1,0:T(1,128)S(1)}, u32[]{:S(2)}, u32[]{:S(2)}) collective-permute-start(f32[8,4,1,256]{3,2,1,0:T(1,128)S(1)} %get-tuple-element.38), channel_id=1, source_target_pairs={{2,0},{4,2},{6,4},{8,6},{10,8},{12,10},{14,12},{16,14},{18,16},{20... | collective-permute-start | bytes 98312 | tf_op jit(solution)/shard_map/ppermute | solution.py:24
  34.3 0.6 collective-permute-done.6
  35.1 0.7 fusion.138
  36.0 5.3 %collective-permute-start.9 = (f32[8,4,2,256]{3,2,1,0:T(2,128)S(1)}, f32[8,4,2,256]{3,2,1,0:T(2,128)S(1)}, u32[]{:S(2)}, u32[]{:S(2)}) collective-permute-start(f32[8,4,2,256]{3,2,1,0:T(2,128)S(1)} %get-tuple-element.36), channel_id=1, source_target_pairs={{2,0},{4,2},{6,4},{8,6},{10,8},{12,10},{14,12},{16,14},{18,16},{20... | collective-permute-start | bytes 196616 | tf_op jit(solution)/shard_map/ppermute | solution.py:24
  41.3 0.6 collective-permute-done.8
  42.4 1.0 fusion.8
  43.5 0.8 fusion.72
  44.4 5.5 %collective-permute-start.13 = (f32[8,4,2,256]{3,2,1,0:T(2,128)S(1)}, f32[8,4,2,256]{3,2,1,0:T(2,128)S(1)}, u32[]{:S(2)}, u32[]{:S(2)}) collective-permute-start(f32[8,4,2,256]{3,2,1,0:T(2,128)S(1)} %get-tuple-element.34), channel_id=1, source_target_pairs={{2,0},{4,2},{6,4},{8,6},{10,8},{12,10},{14,12},{16,14},{18,16},{20... | collective-permute-start | bytes 196616 | tf_op jit(solution)/shard_map/ppermute | solution.py:24
  49.9 0.7 collective-permute-done.12
  51.0 1.0 fusion.16
  52.1 0.8 fusion.80
  53.0 5.7 %collective-permute-start.15 = (f32[8,4,2,256]{3,2,1,0:T(2,128)S(1)}, f32[8,4,2,256]{3,2,1,0:T(2,128)S(1)}, u32[]{:S(2)}, u32[]{:S(2)}) collective-permute-start(f32[8,4,2,256]{3,2,1,0:T(2,128)S(1)} %get-tuple-element.32), channel_id=1, source_target_pairs={{2,0},{4,2},{6,4},{8,6},{10,8},{12,10},{14,12},{16,14},{18,16},{20... | collective-permute-start | bytes 196616 | tf_op jit(solution)/shard_map/ppermute | solution.py:24
  59.8 1.0 fusion.24
  60.9 0.7 fusion.88
  61.7 8.6 %copy.46 = f32[8,4,32,256]{0,3,2,1:T(8,128)} copy(f32[8,4,32,256]{3,2,1,0:T(8,128)S(1)} %fusion.88) | data formatting | bytes 2097152 | tf_op jit(solution)/shard_map/sub | solution.py:80
  70.2 6.5 %gather_fusion = f32[256,8]{1,0:T(8,128)S(1)} fusion(f32[8,32768]{0,1:T(8,128)} %bitcast.35, s32[1024]{0:T(1024)S(1)} %pad_clamp_fusion), kind=kCustom, calls=%fused_computation | custom fusion | bytes 17408 | tf_op jit(solution)/shard_map/jit(_take)/gather | solution.py:97
  77.2 0.7 reshape.115
  78.0 11.3 %all-to-all-start = ((f32[16,1,192]{2,1,0:T(1,128)}), f32[16,1,192]{2,1,0:T(1,128)S(1)}, u32[]{:S(2)}, u32[]{:S(2)}) async-start(f32[16,1,192]{2,1,0:T(1,128)} %reshape.115), calls=%async_computation | async-start | bytes 32768 | tf_op jit(solution)/shard_map/all_to_all | solution.py:102
  89.3 5.8 %all-to-all-done = f32[16,1,192]{2,1,0:T(1,128)S(1)} async-done(((f32[16,1,192]{2,1,0:T(1,128)}), f32[16,1,192]{2,1,0:T(1,128)S(1)}, u32[]{:S(2)}, u32[]{:S(2)}) %all-to-all-start) | async-done | bytes 12320 | tf_op jit(solution)/shard_map/all_to_all | solution.py:102
  95.6 0.7 reduce
  96.5 9.1 %all_to_all.10 = f32[16,1,192]{2,1,0:T(1,128)S(1)} all-to-all(f32[16,1,192]{2,1,0:T(1,128)S(1)} %reshape.117), channel_id=1, replica_groups=mesh['field'=16,'probe'=2] {'field'}, dimensions={0} | all-to-all | bytes 24576 | tf_op jit(solution)/shard_map/all_to_all | solution.py:106
  105.6 0.7 reduce.1
  106.8 8.2 %scatter_custom_fusion = f32[8,32768]{0,1:T(8,128)} fusion(s32[256]{0:T(256)S(1)} %bitcast.43, f32[256,8]{1,0:T(8,128)S(1)} %fusion.154, f32[]{:T(128)} %constant.10.clone.1), kind=kCustom, calls=%fused_computation.2 | custom fusion | flops 2048 | bytes 1048580 | tf_op jit(solution)/shard_map/scatter-add | solution.py:113
  115.1 9.8 %copy.50 = f32[8,4,32,256]{3,2,1,0:T(8,128)S(1)} copy(f32[8,4,32,256]{0,3,2,1:T(8,128)} %bitcast.34) | data formatting | bytes 2097152 | tf_op jit(solution)/shard_map/reshape | solution.py:114
  124.9 0.9 collective-permute-start.16
  125.8 1.3 collective-permute-done.16
  127.1 2.4 %collective-permute-done.17 = f32[8,4,2,256]{3,2,1,0:T(2,128)S(1)} collective-permute-done((f32[8,4,2,256]{3,2,1,0:T(2,128)S(1)}, f32[8,4,2,256]{3,2,1,0:T(2,128)S(1)}, u32[]{:S(2)}, u32[]{:S(2)}) %collective-permute-start.17) | collective-permute-done | bytes 65568 | tf_op jit(solution)/shard_map/ppermute | solution.py:24
  129.9 1.1 broadcast_multiply_fusion.5
  131.1 1.0 fusion.95
  132.3 2.9 %collective-permute-start.19 = (f32[8,4,2,256]{3,2,1,0:T(2,128)S(1)}, f32[8,4,2,256]{3,2,1,0:T(2,128)S(1)}, u32[]{:S(2)}, u32[]{:S(2)}) collective-permute-start(f32[8,4,2,256]{3,2,1,0:T(2,128)S(1)} %get-tuple-element.28), channel_id=1, source_target_pairs={{2,0},{4,2},{6,4},{8,6},{10,8},{12,10},{14,12},{16,14},{18,16},{20... | collective-permute-start | bytes 196616 | tf_op jit(solution)/shard_map/ppermute | solution.py:24
  135.7 1.0 collective-permute-done.19
  137.1 1.1 broadcast_multiply_fusion.4
  138.3 0.9 fusion.102
  139.3 4.9 %collective-permute-start.21 = (f32[8,4,2,256]{3,2,1,0:T(2,128)S(1)}, f32[8,4,2,256]{3,2,1,0:T(2,128)S(1)}, u32[]{:S(2)}, u32[]{:S(2)}) collective-permute-start(f32[8,4,2,256]{3,2,1,0:T(2,128)S(1)} %get-tuple-element.26), channel_id=1, source_target_pairs={{2,0},{4,2},{6,4},{8,6},{10,8},{12,10},{14,12},{16,14},{18,16},{20... | collective-permute-start | bytes 196616 | tf_op jit(solution)/shard_map/ppermute | solution.py:24
  144.2 0.7 collective-permute-done.20
  145.6 1.1 broadcast_multiply_fusion.3
  146.8 1.0 broadcast_divide_fusion
  147.9 5.5 %collective-permute-start.23 = (f32[8,4,1,256]{3,2,1,0:T(1,128)S(1)}, f32[8,4,1,256]{3,2,1,0:T(1,128)S(1)}, u32[]{:S(2)}, u32[]{:S(2)}) collective-permute-start(f32[8,4,1,256]{3,2,1,0:T(1,128)S(1)} %get-tuple-element.24), channel_id=1, source_target_pairs={{2,0},{4,2},{6,4},{8,6},{10,8},{12,10},{14,12},{16,14},{18,16},{20... | collective-permute-start | bytes 98312 | tf_op jit(solution)/shard_map/ppermute | solution.py:24
  153.5 0.6 collective-permute-done.22
  154.3 0.7 fusion.115
  155.2 5.3 %collective-permute-start.25 = (f32[8,4,1,256]{3,2,1,0:T(1,128)S(1)}, f32[8,4,1,256]{3,2,1,0:T(1,128)S(1)}, u32[]{:S(2)}, u32[]{:S(2)}) collective-permute-start(f32[8,4,1,256]{3,2,1,0:T(1,128)S(1)} %get-tuple-element.22), channel_id=1, source_target_pairs={{2,0},{4,2},{6,4},{8,6},{10,8},{12,10},{14,12},{16,14},{18,16},{20... | collective-permute-start | bytes 98312 | tf_op jit(solution)/shard_map/ppermute | solution.py:24
  160.5 0.6 collective-permute-done.24
  161.3 0.7 fusion.121
  162.2 5.3 %collective-permute-start.27 = (f32[8,4,1,256]{3,2,1,0:T(1,128)S(1)}, f32[8,4,1,256]{3,2,1,0:T(1,128)S(1)}, u32[]{:S(2)}, u32[]{:S(2)}) collective-permute-start(f32[8,4,1,256]{3,2,1,0:T(1,128)S(1)} %get-tuple-element.20), channel_id=1, source_target_pairs={{2,0},{4,2},{6,4},{8,6},{10,8},{12,10},{14,12},{16,14},{18,16},{20... | collective-permute-start | bytes 98312 | tf_op jit(solution)/shard_map/ppermute | solution.py:24
  167.5 1.1 copy.54
  168.6 4.4 %psum.15 = f32[16,24]{1,0:T(8,128)S(1)} all-reduce(f32[16,24]{1,0:T(8,128)S(1)} %get-tuple-element.47), channel_id=1, replica_groups=mesh['field'=16,'probe'=2] {'probe'}, use_global_device_ids=true, to_apply=%region_4.5 | all-reduce | flops 384 | bytes 3072 | tf_op jit(solution)/shard_map/psum | solution.py:137
  173.0 0.7 fusion.127
  173.8 5.1 %collective-permute-start.29 = (f32[8,4,1,256]{3,2,1,0:T(1,128)S(1)}, f32[8,4,1,256]{3,2,1,0:T(1,128)S(1)}, u32[]{:S(2)}, u32[]{:S(2)}) collective-permute-start(f32[8,4,1,256]{3,2,1,0:T(1,128)S(1)} %get-tuple-element.18), channel_id=1, source_target_pairs={{2,0},{4,2},{6,4},{8,6},{10,8},{12,10},{14,12},{16,14},{18,16},{20... | collective-permute-start | bytes 98312 | tf_op jit(solution)/shard_map/ppermute | solution.py:24
  178.9 0.6 fusion.165
  179.7 0.7 fusion.133
  180.5 10.8 %all-gather.2.cloned.1.call-done = bf16[16,4,32,256]{3,0,2,1:T(8,128)(2,1)} async-done(((bf16[8,4,32,256]{3,0,2,1:T(8,128)(2,1)}), bf16[16,4,32,256]{3,0,2,1:T(8,128)(2,1)}) %all-gather.2.cloned.1.call-update) | async-done | bytes 1048592 | tf_op jit(solution)/shard_map/all_gather | solution.py:129
  191.3 2.9 %convolution_bitcast_fusion = f32[8,16]{1,0:T(8,128)S(1)} fusion(bf16[16,4,32,256]{3,0,2,1:T(8,128)(2,1)} %all-gather.2.cloned.1.call-done, f32[8,4,32,256]{3,2,1,0:T(8,128)S(1)} %fusion.133), kind=kOutput, calls=%fused_computation.158 | convolution fusion | flops 50331648 | bytes 2097664 | tf_op jit(solution)/shard_map/dot_general | solution.py:131
  194.2 29.7 %psum.14 = f32[8,16]{1,0:T(8,128)S(1)} all-reduce(f32[8,16]{1,0:T(8,128)S(1)} %convolution_bitcast_fusion), channel_id=1, replica_groups=mesh['field'=16,'probe'=2] {'field'}, use_global_device_ids=true, to_apply=%region_2.3 | all-reduce | flops 128 | bytes 1024 | tf_op jit(solution)/shard_map/psum | solution.py:135
  223.9 0.6 broadcast_multiply_fusion.7
  (100 shorter events, 10.5 us)
Async XLA Ops:
  7.2 8.6 %copy-start = (bf16[8,4,32,256]{3,2,1,0:T(8,128)(2,1)S(1)}, bf16[8,4,32,256]{3,2,1,0:T(8,128)(2,1)}, u32[]{:S(2)}) copy-start(bf16[8,4,32,256]{3,2,1,0:T(8,128)(2,1)} %param.8) | copy-start | bytes 1572868
  7.2 4.9 %copy-start.2 = (f32[4,32,256]{2,1,0:T(8,128)S(1)}, f32[4,32,256]{2,1,0:T(8,128)}, u32[]{:S(2)}) copy-start(f32[4,32,256]{2,1,0:T(8,128)} %param.10) | copy-start | bytes 393220
  9.4 5.8 %collective-permute-start = (f32[8,4,1,256]{3,2,1,0:T(1,128)S(1)}, f32[8,4,1,256]{3,2,1,0:T(1,128)S(1)}, u32[]{:S(2)}, u32[]{:S(2)}) collective-permute-start(f32[8,4,1,256]{3,2,1,0:T(1,128)S(1)} %get-tuple-element.43), channel_id=1, source_target_pairs={{0,2},{2,4},{4,6},{6,8},{8,10},{10,12},{12,14},{14,16},{16,18},{18... | collective-permute-start | bytes 98312 | tf_op jit(solution)/shard_map/ppermute | solution.py:23
  12.1 3.6 %collective-permute-start.1 = (f32[8,4,1,256]{3,2,1,0:T(1,128)S(1)}, f32[8,4,1,256]{3,2,1,0:T(1,128)S(1)}, u32[]{:S(2)}, u32[]{:S(2)}) collective-permute-start(f32[8,4,1,256]{3,2,1,0:T(1,128)S(1)} %get-tuple-element.44), channel_id=1, source_target_pairs={{2,0},{4,2},{6,4},{8,6},{10,8},{12,10},{14,12},{16,14},{18,16},{20... | collective-permute-start | bytes 98312 | tf_op jit(solution)/shard_map/ppermute | solution.py:24
  12.1 29.2 %collective-permute-start.10 = (f32[4,2,256]{2,1,0:T(2,128)S(1)}, f32[4,2,256]{2,1,0:T(2,128)S(1)}, u32[]{:S(2)}, u32[]{:S(2)}) collective-permute-start(f32[4,2,256]{2,1,0:T(2,128)S(1)} %get-tuple-element.45), channel_id=1, source_target_pairs={{0,2},{2,4},{4,6},{6,8},{8,10},{10,12},{12,14},{14,16},{16,18},{18... | collective-permute-start | bytes 24584 | tf_op jit(solution)/shard_map/ppermute | solution.py:23
  13.9 6.5 %copy-start.5 = (s32[1,256,1]{1,2,0:T(1,128)S(1)}, s32[1,256,1]{1,2,0:T(1,128)}, u32[]{:S(2)}) copy-start(s32[1,256,1]{1,2,0:T(1,128)} %param.13) | copy-start | bytes 3076
  13.9 27.4 %collective-permute-start.11 = (f32[4,2,256]{2,1,0:T(2,128)S(1)}, f32[4,2,256]{2,1,0:T(2,128)S(1)}, u32[]{:S(2)}, u32[]{:S(2)}) collective-permute-start(f32[4,2,256]{2,1,0:T(2,128)S(1)} %get-tuple-element.46), channel_id=1, source_target_pairs={{2,0},{4,2},{6,4},{8,6},{10,8},{12,10},{14,12},{16,14},{18,16},{20... | collective-permute-start | bytes 24584 | tf_op jit(solution)/shard_map/ppermute | solution.py:24
  16.5 4.6 %collective-permute-start.2 = (f32[8,4,1,256]{3,2,1,0:T(1,128)S(1)}, f32[8,4,1,256]{3,2,1,0:T(1,128)S(1)}, u32[]{:S(2)}, u32[]{:S(2)}) collective-permute-start(f32[8,4,1,256]{3,2,1,0:T(1,128)S(1)} %get-tuple-element.41), channel_id=1, source_target_pairs={{0,2},{2,4},{4,6},{6,8},{8,10},{10,12},{12,14},{14,16},{16,18},{18... | collective-permute-start | bytes 98312 | tf_op jit(solution)/shard_map/ppermute | solution.py:23
  16.6 4.7 %collective-permute-start.3 = (f32[8,4,1,256]{3,2,1,0:T(1,128)S(1)}, f32[8,4,1,256]{3,2,1,0:T(1,128)S(1)}, u32[]{:S(2)}, u32[]{:S(2)}) collective-permute-start(f32[8,4,1,256]{3,2,1,0:T(1,128)S(1)} %get-tuple-element.42), channel_id=1, source_target_pairs={{2,0},{4,2},{6,4},{8,6},{10,8},{12,10},{14,12},{16,14},{18,16},{20... | collective-permute-start | bytes 98312 | tf_op jit(solution)/shard_map/ppermute | solution.py:24
  22.1 5.9 %collective-permute-start.4 = (f32[8,4,1,256]{3,2,1,0:T(1,128)S(1)}, f32[8,4,1,256]{3,2,1,0:T(1,128)S(1)}, u32[]{:S(2)}, u32[]{:S(2)}) collective-permute-start(f32[8,4,1,256]{3,2,1,0:T(1,128)S(1)} %get-tuple-element.39), channel_id=1, source_target_pairs={{0,2},{2,4},{4,6},{6,8},{8,10},{10,12},{12,14},{14,16},{16,18},{18... | collective-permute-start | bytes 98312 | tf_op jit(solution)/shard_map/ppermute | solution.py:23
  22.1 6.0 %collective-permute-start.5 = (f32[8,4,1,256]{3,2,1,0:T(1,128)S(1)}, f32[8,4,1,256]{3,2,1,0:T(1,128)S(1)}, u32[]{:S(2)}, u32[]{:S(2)}) collective-permute-start(f32[8,4,1,256]{3,2,1,0:T(1,128)S(1)} %get-tuple-element.40), channel_id=1, source_target_pairs={{2,0},{4,2},{6,4},{8,6},{10,8},{12,10},{14,12},{16,14},{18,16},{20... | collective-permute-start | bytes 98312 | tf_op jit(solution)/shard_map/ppermute | solution.py:24
  28.0 6.3 %copy-start.6 = (s32[1,256]{1,0:T(1,128)S(1)}, s32[1,256]{1,0:T(1,128)}, u32[]{:S(2)}) copy-start(s32[1,256]{1,0:T(1,128)} %param.12) | copy-start | bytes 3076
  28.9 6.0 %collective-permute-start.6 = (f32[8,4,1,256]{3,2,1,0:T(1,128)S(1)}, f32[8,4,1,256]{3,2,1,0:T(1,128)S(1)}, u32[]{:S(2)}, u32[]{:S(2)}) collective-permute-start(f32[8,4,1,256]{3,2,1,0:T(1,128)S(1)} %get-tuple-element.37), channel_id=1, source_target_pairs={{0,2},{2,4},{4,6},{6,8},{8,10},{10,12},{12,14},{14,16},{16,18},{18... | collective-permute-start | bytes 98312 | tf_op jit(solution)/shard_map/ppermute | solution.py:23
  29.0 6.1 %collective-permute-start.7 = (f32[8,4,1,256]{3,2,1,0:T(1,128)S(1)}, f32[8,4,1,256]{3,2,1,0:T(1,128)S(1)}, u32[]{:S(2)}, u32[]{:S(2)}) collective-permute-start(f32[8,4,1,256]{3,2,1,0:T(1,128)S(1)} %get-tuple-element.38), channel_id=1, source_target_pairs={{2,0},{4,2},{6,4},{8,6},{10,8},{12,10},{14,12},{16,14},{18,16},{20... | collective-permute-start | bytes 98312 | tf_op jit(solution)/shard_map/ppermute | solution.py:24
  35.9 6.0 %collective-permute-start.8 = (f32[8,4,2,256]{3,2,1,0:T(2,128)S(1)}, f32[8,4,2,256]{3,2,1,0:T(2,128)S(1)}, u32[]{:S(2)}, u32[]{:S(2)}) collective-permute-start(f32[8,4,2,256]{3,2,1,0:T(2,128)S(1)} %get-tuple-element.35), channel_id=1, source_target_pairs={{0,2},{2,4},{4,6},{6,8},{8,10},{10,12},{12,14},{14,16},{16,18},{18... | collective-permute-start | bytes 196616 | tf_op jit(solution)/shard_map/ppermute | solution.py:23
  36.0 6.2 %collective-permute-start.9 = (f32[8,4,2,256]{3,2,1,0:T(2,128)S(1)}, f32[8,4,2,256]{3,2,1,0:T(2,128)S(1)}, u32[]{:S(2)}, u32[]{:S(2)}) collective-permute-start(f32[8,4,2,256]{3,2,1,0:T(2,128)S(1)} %get-tuple-element.36), channel_id=1, source_target_pairs={{2,0},{4,2},{6,4},{8,6},{10,8},{12,10},{14,12},{16,14},{18,16},{20... | collective-permute-start | bytes 196616 | tf_op jit(solution)/shard_map/ppermute | solution.py:24
  44.3 6.3 %collective-permute-start.12 = (f32[8,4,2,256]{3,2,1,0:T(2,128)S(1)}, f32[8,4,2,256]{3,2,1,0:T(2,128)S(1)}, u32[]{:S(2)}, u32[]{:S(2)}) collective-permute-start(f32[8,4,2,256]{3,2,1,0:T(2,128)S(1)} %get-tuple-element.33), channel_id=1, source_target_pairs={{0,2},{2,4},{4,6},{6,8},{8,10},{10,12},{12,14},{14,16},{16,18},{18... | collective-permute-start | bytes 196616 | tf_op jit(solution)/shard_map/ppermute | solution.py:23
  44.4 6.4 %collective-permute-start.13 = (f32[8,4,2,256]{3,2,1,0:T(2,128)S(1)}, f32[8,4,2,256]{3,2,1,0:T(2,128)S(1)}, u32[]{:S(2)}, u32[]{:S(2)}) collective-permute-start(f32[8,4,2,256]{3,2,1,0:T(2,128)S(1)} %get-tuple-element.34), channel_id=1, source_target_pairs={{2,0},{4,2},{6,4},{8,6},{10,8},{12,10},{14,12},{16,14},{18,16},{20... | collective-permute-start | bytes 196616 | tf_op jit(solution)/shard_map/ppermute | solution.py:24
  52.9 6.3 %collective-permute-start.14 = (f32[8,4,2,256]{3,2,1,0:T(2,128)S(1)}, f32[8,4,2,256]{3,2,1,0:T(2,128)S(1)}, u32[]{:S(2)}, u32[]{:S(2)}) collective-permute-start(f32[8,4,2,256]{3,2,1,0:T(2,128)S(1)} %get-tuple-element.31), channel_id=1, source_target_pairs={{0,2},{2,4},{4,6},{6,8},{8,10},{10,12},{12,14},{14,16},{16,18},{18... | collective-permute-start | bytes 196616 | tf_op jit(solution)/shard_map/ppermute | solution.py:23
  53.0 6.6 %collective-permute-start.15 = (f32[8,4,2,256]{3,2,1,0:T(2,128)S(1)}, f32[8,4,2,256]{3,2,1,0:T(2,128)S(1)}, u32[]{:S(2)}, u32[]{:S(2)}) collective-permute-start(f32[8,4,2,256]{3,2,1,0:T(2,128)S(1)} %get-tuple-element.32), channel_id=1, source_target_pairs={{2,0},{4,2},{6,4},{8,6},{10,8},{12,10},{14,12},{16,14},{18,16},{20... | collective-permute-start | bytes 196616 | tf_op jit(solution)/shard_map/ppermute | solution.py:24
  61.6 27.6 %copy-start.3 = (f32[1,16,24]{2,1,0:T(8,128)S(1)}, f32[1,16,24]{2,1,0:T(8,128)}, u32[]{:S(2)}) copy-start(f32[1,16,24]{2,1,0:T(8,128)} %param.15) | copy-start | bytes 4612
  61.6 27.6 %copy-start.4 = (f32[1,16,24]{2,1,0:T(8,128)S(1)}, f32[1,16,24]{2,1,0:T(8,128)}, u32[]{:S(2)}) copy-start(f32[1,16,24]{2,1,0:T(8,128)} %param.14) | copy-start | bytes 4612
  78.0 17.1 %all-to-all-start = ((f32[16,1,192]{2,1,0:T(1,128)}), f32[16,1,192]{2,1,0:T(1,128)S(1)}, u32[]{:S(2)}, u32[]{:S(2)}) async-start(f32[16,1,192]{2,1,0:T(1,128)} %reshape.115), calls=%async_computation | async-start | bytes 32768 | tf_op jit(solution)/shard_map/all_to_all | solution.py:102
  89.2 102.1 %all-gather.2.cloned.1.call-start = ((), (), s32[]{:S(2)}) async-start(), calls=%async_computation.2 | async-start | bytes 1572864 | tf_op jit(solution)/shard_map/all_gather | solution.py:129
  124.9 2.2 collective-permute-start.16
  125.8 3.7 %collective-permute-start.17 = (f32[8,4,2,256]{3,2,1,0:T(2,128)S(1)}, f32[8,4,2,256]{3,2,1,0:T(2,128)S(1)}, u32[]{:S(2)}, u32[]{:S(2)}) collective-permute-start(f32[8,4,2,256]{3,2,1,0:T(2,128)S(1)} %get-tuple-element.30), channel_id=1, source_target_pairs={{2,0},{4,2},{6,4},{8,6},{10,8},{12,10},{14,12},{16,14},{18,16},{20... | collective-permute-start | bytes 196616 | tf_op jit(solution)/shard_map/ppermute | solution.py:24
  132.2 3.5 %collective-permute-start.18 = (f32[8,4,2,256]{3,2,1,0:T(2,128)S(1)}, f32[8,4,2,256]{3,2,1,0:T(2,128)S(1)}, u32[]{:S(2)}, u32[]{:S(2)}) collective-permute-start(f32[8,4,2,256]{3,2,1,0:T(2,128)S(1)} %get-tuple-element.27), channel_id=1, source_target_pairs={{0,2},{2,4},{4,6},{6,8},{8,10},{10,12},{12,14},{14,16},{16,18},{18... | collective-permute-start | bytes 196616 | tf_op jit(solution)/shard_map/ppermute | solution.py:23
  132.3 4.4 %collective-permute-start.19 = (f32[8,4,2,256]{3,2,1,0:T(2,128)S(1)}, f32[8,4,2,256]{3,2,1,0:T(2,128)S(1)}, u32[]{:S(2)}, u32[]{:S(2)}) collective-permute-start(f32[8,4,2,256]{3,2,1,0:T(2,128)S(1)} %get-tuple-element.28), channel_id=1, source_target_pairs={{2,0},{4,2},{6,4},{8,6},{10,8},{12,10},{14,12},{16,14},{18,16},{20... | collective-permute-start | bytes 196616 | tf_op jit(solution)/shard_map/ppermute | solution.py:24
  139.3 5.7 %collective-permute-start.20 = (f32[8,4,2,256]{3,2,1,0:T(2,128)S(1)}, f32[8,4,2,256]{3,2,1,0:T(2,128)S(1)}, u32[]{:S(2)}, u32[]{:S(2)}) collective-permute-start(f32[8,4,2,256]{3,2,1,0:T(2,128)S(1)} %get-tuple-element.25), channel_id=1, source_target_pairs={{0,2},{2,4},{4,6},{6,8},{8,10},{10,12},{12,14},{14,16},{16,18},{18... | collective-permute-start | bytes 196616 | tf_op jit(solution)/shard_map/ppermute | solution.py:23
  139.3 5.8 %collective-permute-start.21 = (f32[8,4,2,256]{3,2,1,0:T(2,128)S(1)}, f32[8,4,2,256]{3,2,1,0:T(2,128)S(1)}, u32[]{:S(2)}, u32[]{:S(2)}) collective-permute-start(f32[8,4,2,256]{3,2,1,0:T(2,128)S(1)} %get-tuple-element.26), channel_id=1, source_target_pairs={{2,0},{4,2},{6,4},{8,6},{10,8},{12,10},{14,12},{16,14},{18,16},{20... | collective-permute-start | bytes 196616 | tf_op jit(solution)/shard_map/ppermute | solution.py:24
  147.9 6.2 %collective-permute-start.22 = (f32[8,4,1,256]{3,2,1,0:T(1,128)S(1)}, f32[8,4,1,256]{3,2,1,0:T(1,128)S(1)}, u32[]{:S(2)}, u32[]{:S(2)}) collective-permute-start(f32[8,4,1,256]{3,2,1,0:T(1,128)S(1)} %get-tuple-element.23), channel_id=1, source_target_pairs={{0,2},{2,4},{4,6},{6,8},{8,10},{10,12},{12,14},{14,16},{16,18},{18... | collective-permute-start | bytes 98312 | tf_op jit(solution)/shard_map/ppermute | solution.py:23
  147.9 6.4 %collective-permute-start.23 = (f32[8,4,1,256]{3,2,1,0:T(1,128)S(1)}, f32[8,4,1,256]{3,2,1,0:T(1,128)S(1)}, u32[]{:S(2)}, u32[]{:S(2)}) collective-permute-start(f32[8,4,1,256]{3,2,1,0:T(1,128)S(1)} %get-tuple-element.24), channel_id=1, source_target_pairs={{2,0},{4,2},{6,4},{8,6},{10,8},{12,10},{14,12},{16,14},{18,16},{20... | collective-permute-start | bytes 98312 | tf_op jit(solution)/shard_map/ppermute | solution.py:24
  155.1 6.0 %collective-permute-start.24 = (f32[8,4,1,256]{3,2,1,0:T(1,128)S(1)}, f32[8,4,1,256]{3,2,1,0:T(1,128)S(1)}, u32[]{:S(2)}, u32[]{:S(2)}) collective-permute-start(f32[8,4,1,256]{3,2,1,0:T(1,128)S(1)} %get-tuple-element.21), channel_id=1, source_target_pairs={{0,2},{2,4},{4,6},{6,8},{8,10},{10,12},{12,14},{14,16},{16,18},{18... | collective-permute-start | bytes 98312 | tf_op jit(solution)/shard_map/ppermute | solution.py:23
  155.2 6.2 %collective-permute-start.25 = (f32[8,4,1,256]{3,2,1,0:T(1,128)S(1)}, f32[8,4,1,256]{3,2,1,0:T(1,128)S(1)}, u32[]{:S(2)}, u32[]{:S(2)}) collective-permute-start(f32[8,4,1,256]{3,2,1,0:T(1,128)S(1)} %get-tuple-element.22), channel_id=1, source_target_pairs={{2,0},{4,2},{6,4},{8,6},{10,8},{12,10},{14,12},{16,14},{18,16},{20... | collective-permute-start | bytes 98312 | tf_op jit(solution)/shard_map/ppermute | solution.py:24
  162.1 10.9 %collective-permute-start.26 = (f32[8,4,1,256]{3,2,1,0:T(1,128)S(1)}, f32[8,4,1,256]{3,2,1,0:T(1,128)S(1)}, u32[]{:S(2)}, u32[]{:S(2)}) collective-permute-start(f32[8,4,1,256]{3,2,1,0:T(1,128)S(1)} %get-tuple-element.19), channel_id=1, source_target_pairs={{0,2},{2,4},{4,6},{6,8},{8,10},{10,12},{12,14},{14,16},{16,18},{18... | collective-permute-start | bytes 98312 | tf_op jit(solution)/shard_map/ppermute | solution.py:23
  162.2 10.8 %collective-permute-start.27 = (f32[8,4,1,256]{3,2,1,0:T(1,128)S(1)}, f32[8,4,1,256]{3,2,1,0:T(1,128)S(1)}, u32[]{:S(2)}, u32[]{:S(2)}) collective-permute-start(f32[8,4,1,256]{3,2,1,0:T(1,128)S(1)} %get-tuple-element.20), channel_id=1, source_target_pairs={{2,0},{4,2},{6,4},{8,6},{10,8},{12,10},{14,12},{16,14},{18,16},{20... | collective-permute-start | bytes 98312 | tf_op jit(solution)/shard_map/ppermute | solution.py:24
  173.7 5.8 %collective-permute-start.28 = (f32[8,4,1,256]{3,2,1,0:T(1,128)S(1)}, f32[8,4,1,256]{3,2,1,0:T(1,128)S(1)}, u32[]{:S(2)}, u32[]{:S(2)}) collective-permute-start(f32[8,4,1,256]{3,2,1,0:T(1,128)S(1)} %get-tuple-element.17), channel_id=1, source_target_pairs={{0,2},{2,4},{4,6},{6,8},{8,10},{10,12},{12,14},{14,16},{16,18},{18... | collective-permute-start | bytes 98312 | tf_op jit(solution)/shard_map/ppermute | solution.py:23
  173.8 6.0 %collective-permute-start.29 = (f32[8,4,1,256]{3,2,1,0:T(1,128)S(1)}, f32[8,4,1,256]{3,2,1,0:T(1,128)S(1)}, u32[]{:S(2)}, u32[]{:S(2)}) collective-permute-start(f32[8,4,1,256]{3,2,1,0:T(1,128)S(1)} %get-tuple-element.18), channel_id=1, source_target_pairs={{2,0},{4,2},{6,4},{8,6},{10,8},{12,10},{14,12},{16,14},{18,16},{20... | collective-permute-start | bytes 98312 | tf_op jit(solution)/shard_map/ppermute | solution.py:24
  180.5 44.0 %copy-start.1 = (f32[8,4,32,256]{3,2,1,0:T(8,128)}, f32[8,4,32,256]{3,2,1,0:T(8,128)S(1)}, u32[]{:S(2)}) copy-start(f32[8,4,32,256]{3,2,1,0:T(8,128)S(1)} %fusion.133) | copy-start | bytes 3145732
Sparse Core Ops, SparseCore 0:
  168.7 22.5 all-gather.1
where the time goes:
time: 236 us; the launch traced here: 231 us
  starting transfers between devices  78.5 us (33%)
  blocking collectives  43.1 us (18%)
  other arithmetic  31.7 us (13%)
  waiting for transfers between devices  29.6 us (13%)
  local copies, waits for them, and re-layouts  29.5 us (12%)
  between operations  15.3 us (6%)
  matrix products  3.61 us (2%)
    ppermute x15, starting transfers between devices, with_halo(): after = lax.ppermute(first, axis, down)  61.2 us
    psum x1, blocking collectives, on_device(): tiles = lax.psum(columns, 'field') * scale_factor  29.7 us
    all_to_all x1, starting transfers between devices, on_device(): lax.all_to_all(outgoing, 'field', split_axis=0, concat_axis=0, tiled=True)  11.3 us
    all_gather x1, waiting for transfers between devices, on_device(): piece = lax.all_gather(probes, 'probe', axis=0, tiled=True)  10.8 us
    reshape x1, local copies, waits for them, and re-layouts, on_device(): adjoint = injected.reshape(probes.shape)  9.83 us
    all_to_all x1, blocking collectives, on_device(): lax.all_to_all(weighted, 'field', split_axis=0, concat_axis=0, tiled=True)  9.07 us
    sub x1, local copies, waits for them, and re-layouts, on_device(): middle + coef_mid * (beside_all - 6.0 * middle)  8.58 us
    scatter-add x1, other arithmetic, on_device(): jnp.zeros((probe_count, cell_count), jnp.float32).at[:, cells]  8.2 us
  transfers between devices with their start and end apart: 32, of which 25 were waited for; matrix products, arithmetic and copies ran while one was open for 3% of the time, Pallas kernels for 0%

commit v1 on v0

v1 whole, which is shorter than its diff:
```python
import functools
import math

import jax
import jax.numpy as jnp
from jax import lax
from jax.experimental import pallas as pl
from jax.experimental.pallas import tpu as pltpu
from jax.sharding import PartitionSpec as P

SWEEPS = 4
STEPS = 6
HALO = SWEEPS + STEPS
SENS_DEV = 160
ADVECT = 0.3
LANES = 128
F32 = jnp.float32
HIGHEST = lax.Precision.HIGHEST


def rows_of(ref, row, per):
    block = ref[pl.ds(row * per, per)]
    return [block[i].astype(F32) for i in range(per)]


def put_rows(ref, row, per, values):
    for i in range(per):
        ref[row * per + i] = values[i]


def around(west, mid, east, halves, at_first, at_last):
    per = len(mid)
    zero = jnp.zeros_like(mid[0])
    fwd = [pltpu.roll(t, 1, 1) for t in mid]
    bwd = [pltpu.roll(t, LANES - 1, 1) for t in mid]
    out = []
    for i in range(per):
        half = i % halves
        prev = fwd[i - 1] if half > 0 else zero
        following = bwd[i + 1] if half < halves - 1 else zero
        side = jnp.where(at_first, prev, fwd[i]) + jnp.where(at_last, following, bwd[i])
        total = (west[i] + east[i]) + side
        depth = [mid[j] for j in (i - halves, i + halves) if 0 <= j < per]
        if len(depth) == 2:
            total = total + (depth[0] + depth[1])
        elif depth:
            total = total + depth[0]
        out.append(total)
    return out


def kernel(
    dims,
    p_in,
    c_in,
    cell_s,
    count_s,
    cell_v,
    owner_v,
    logit,
    noise,
    h_out,
    t_out,
    g_out,
    src,
    coef,
    kap,
    rec,
    buf_a,
    buf_b,
    inj,
    wpad,
    wsend,
    wrecv,
    wfield,
    obs,
    msend,
    mrecv,
    sq2d,
    local_sem,
    halo_send,
    halo_recv,
    w_send,
    w_recv,
    o_send,
    o_recv,
    m_send,
    m_recv,
):
    nf, npr, nz, cx, ny, cap, slots = dims
    halves = ny // LANES
    per = nz * halves
    wide = cx + 2 * HALO
    end = HALO + cx
    me = lax.axis_index("field")
    mine = lax.axis_index("probe")
    left = lax.rem(me + nf - 1, nf)
    right = lax.rem(me + 1, nf)

    own_p = pltpu.make_async_copy(p_in, src.at[pl.ds(HALO * per, cx * per)], local_sem.at[0])
    own_c = pltpu.make_async_copy(c_in, coef.at[pl.ds(HALO, cx)], local_sem.at[1])
    own_p.start()
    own_c.start()

    barrier = pltpu.get_barrier_semaphore()
    for j in range(1, nf):
        pl.semaphore_signal(
            barrier,
            inc=1,
            device_id={"field": lax.rem(me + j, nf)},
            device_id_type=pl.DeviceIdType.MESH,
        )
    for j in range(1, npr):
        pl.semaphore_signal(
            barrier,
            inc=1,
            device_id={"probe": lax.rem(mine + j, npr)},
            device_id_type=pl.DeviceIdType.MESH,
        )
    pl.semaphore_wait(barrier, nf + npr - 2)

    def send(source, target, send_sem, recv_sem, where):
        return pltpu.make_async_remote_copy(
            src_ref=source,
            dst_ref=target,
            send_sem=send_sem,
            recv_sem=recv_sem,
            device_id=where,
            device_id_type=pl.DeviceIdType.MESH,
        )

    def halo_pair(source, source_row, target, scale, first):
        to_right = send(
            source.at[pl.ds((source_row + cx - HALO) * scale, HALO * scale)],
            target.at[pl.ds(0, HALO * scale)],
            halo_send.at[first],
            halo_recv.at[first],
            {"field": right},
        )
        to_left = send(
            source.at[pl.ds(source_row * scale, HALO * scale)],
            target.at[pl.ds(end * scale, HALO * scale)],
            halo_send.at[first + 1],
            halo_recv.at[first + 1],
            {"field": left},
        )
        to_right.start()
        to_left.start()
        return [to_right, to_left]

    edge_c = halo_pair(c_in, 0, coef, 1, 0)
    edge_p = halo_pair(p_in, 0, src, per, 2)

    gated = jax.nn.sigmoid(logit[...])
    wpad[...] = jnp.zeros_like(wpad)
    wpad[:, :cap] = gated * noise[...]
    for b in range(nf):
        wsend[b] = jnp.broadcast_to(wpad[b : b + 1, :], (8, LANES))
    wrecv[me] = wsend[me]
    w_copies = []
    for j in range(1, nf):
        other = lax.rem(me + j, nf)
        copy = send(
            wsend.at[other], wrecv.at[me], w_send.at[j - 1], w_recv.at[j - 1], {"field": other}
        )
        copy.start()
        w_copies.append(copy)

    sub = lax.broadcasted_iota(jnp.int32, (slots, slots), 0)
    lan = lax.broadcasted_iota(jnp.int32, (slots, slots), 1)
    eye = sub == lan

    def column(row):
        return jnp.sum(jnp.where(eye, row, 0.0), axis=1, keepdims=True)

    cell = cell_v[...]
    shift_x = ny.bit_length() - 1
    shift_z = shift_x + cx.bit_length() - 1
    line_row = ((cell >> shift_x) & (cx - 1)) * nz + (cell >> shift_z)
    owner_row = owner_v[...].astype(F32)
    y_col = column((cell & (ny - 1)).astype(F32))
    owner_col = column(owner_row)
    pos_col = jnp.sum(
        jnp.where(jnp.logical_and(owner_col == owner_row, lan < sub), 1.0, 0.0),
        axis=1,
        keepdims=True,
    )
    count = count_s[0]
    lane_pos = lax.broadcasted_iota(jnp.int32, (slots, LANES), 1).astype(F32)
    pos_hot = lane_pos == pos_col

    own_c.wait()
    own_p.wait()

    def spread(x, carry):
        tile = coef[x]
        for z in range(nz):
            for h in range(halves):
                at = slice(h * LANES, (h + 1) * LANES)
                kap[x * per + z * halves + h] = jnp.broadcast_to(tile[z : z + 1, at], (8, LANES))
                rec[x * per + z * halves + h] = 1.0 / jnp.broadcast_to(
                    tile[nz + z : nz + z + 1, at] + 6.0, (8, LANES)
                )
        return carry

    lax.fori_loop(HALO, end, spread, 0)
    for copy in edge_c:
        copy.wait()
    lax.fori_loop(0, HALO, spread, 0)
    lax.fori_loop(end, wide, spread, 0)

    lane = lax.broadcasted_iota(jnp.int32, (8, LANES), 1)
    at_first = lane == 0
    at_last = lane == LANES - 1
    ring = functools.partial(around, halves=halves, at_first=at_first, at_last=at_last)
    span = range(per)

    def prior(origin, out_first, out_last, buffers):
        def start(row):
            s = rows_of(origin, row, per)
            r = rows_of(rec, row, per)
            return [s[i] * r[i] for i in span]

        reach = SWEEPS
        for sweep in range(SWEEPS):
            reach -= 1
            first, last = out_first - reach, out_last + reach
            target, target_row = buffers[sweep + 1]
            if sweep == 0:
                load = start
            else:
                load = functools.partial(rows_of, buffers[sweep][0], per=per)

            def body(x, carry, load=load, target=target, target_row=target_row):
                west, mid = carry[:per], carry[per:]
                east = load(x + 1)
                ring_sum = ring(west, mid, east)
                s = rows_of(origin, x, per)
                r = rows_of(rec, x, per)
                put_rows(target, x - target_row, per, [(s[i] + ring_sum[i]) * r[i] for i in span])
                return tuple(mid) + tuple(east)

            lax.fori_loop(
                first, last, body, tuple(load(first - 1)) + tuple(load(first)), unroll=2
            )

    for copy in edge_p:
        copy.wait()
    flip = ((None, 0), (buf_a, 0), (buf_b, 0), (buf_a, 0), (buf_b, 0))
    prior(src, HALO - STEPS, end + STEPS, flip)

    for step in range(STEPS):
        u, new = (buf_b, buf_a) if step % 2 == 0 else (buf_a, buf_b)
        reach = STEPS - 1 - step

        def body(x, carry, u=u, new=new):
            west, mid = carry[:per], carry[per:]
            east = rows_of(u, x + 1, per)
            ring_sum = ring(west, mid, east)
            k = rows_of(kap, x, per)
            put_rows(
                new,
                x,
                per,
                [
                    k[i] * ring_sum[i]
                    + ((1.0 - ADVECT) - 6.0 * k[i]) * mid[i]
                    + ADVECT * west[i]
                    for i in span
                ],
            )
            return tuple(mid) + tuple(east)

        first, last = HALO - reach, end + reach
        lax.fori_loop(
            first,
            last,
            body,
            tuple(rows_of(u, first - 1, per)) + tuple(rows_of(u, first, per)),
            unroll=2,
        )
    state = buf_b if STEPS % 2 == 0 else buf_a
    spare = buf_a if STEPS % 2 == 0 else buf_b

    for copy in w_copies:
        copy.wait()
    chosen = jnp.zeros((slots, LANES), F32)
    for o in range(nf):
        chosen = jnp.where(owner_col == float(o), wrecv[o][0:1, :], chosen)
    live_col = lax.broadcasted_iota(jnp.int32, (slots, 1), 0) < count
    weight_col = jnp.sum(jnp.where(pos_hot, chosen, 0.0), axis=1, keepdims=True)
    weight_col = jnp.where(live_col, weight_col, 0.0)
    line_iota = lax.broadcasted_iota(jnp.int32, (cx * nz, slots), 0)
    line_hot = jnp.where(line_iota == line_row, 1.0, 0.0)
    lane_y = lax.broadcasted_iota(jnp.int32, (slots, ny), 1).astype(F32)
    y_weight = jnp.where(lane_y == y_col, weight_col, 0.0)
    wfield[...] = jnp.dot(line_hot, y_weight, precision=HIGHEST, preferred_element_type=F32)
    weight_row = jnp.sum(jnp.where(eye, weight_col, 0.0), axis=0, keepdims=True)

    group = 8 // nz

    def inject(g, carry):
        tile = wfield[pl.ds(pl.multiple_of(g * 8, 8), 8), :]
        for r in range(8):
            for h in range(halves):
                at = (HALO + g * group + r // nz) * per + (r % nz) * halves + h
                w = jnp.broadcast_to(tile[r : r + 1, h * LANES : (h + 1) * LANES], (8, LANES))
                inj[at] = state[at] * w
        return carry

    lax.fori_loop(0, cx // group, inject, 0)
    edge_v = halo_pair(inj, HALO, inj, per, 4)

    for part in range(slots // LANES):

        def pick(s, held, part=part):
            c = cell_s[0, part * LANES + s]
            y = c & (ny - 1)
            at = (HALO + ((c >> shift_x) & (cx - 1))) * per
            at = at + (c >> shift_z) * halves + (y >> 7)
            turn = (s - y) & (LANES - 1)
            return jnp.where(lane == s, pltpu.roll(state[at], turn, 1), held)

        held = lax.fori_loop(0, LANES, pick, jnp.zeros((8, LANES), F32), unroll=8)
        held = jnp.where(lane + part * LANES < count, held, 0.0)
        obs[mine, :, part * LANES : (part + 1) * LANES] = held
    o_copies = []
    for j in range(1, npr):
        other = lax.rem(mine + j, npr)
        copy = send(
            obs.at[mine], obs.at[mine], o_send.at[j - 1], o_recv.at[j - 1], {"probe": other}
        )
        copy.start()
        o_copies.append(copy)

    for copy in edge_v:
        copy.wait()

    def adjoint_steps(lo, hi, v):
        for step in range(lo, hi):
            new = spare if step % 2 == 0 else state

            def body(x, carry, v=v, new=new):
                q_west, q_mid, mid = carry[:per], carry[per : 2 * per], carry[2 * per :]
                east = rows_of(v, x + 1, per)
                k = rows_of(kap, x + 1, per)
                q_east = [k[i] * east[i] for i in span]
                ring_sum = ring(q_west, q_mid, q_east)
                put_rows(
                    new,
                    x,
                    per,
                    [
                        (ring_sum[i] - 6.0 * q_mid[i])
                        + ((1.0 - ADVECT) * mid[i] + ADVECT * east[i])
                        for i in span
                    ],
                )
                return tuple(q_mid) + tuple(q_east) + tuple(east)

            first, last = step + 1, wide - step - 1
            v0, v1 = rows_of(v, first - 1, per), rows_of(v, first, per)
            k0, k1 = rows_of(kap, first - 1, per), rows_of(kap, first, per)
            q0 = [k0[i] * v0[i] for i in span]
            q1 = [k1[i] * v1[i] for i in span]
            lax.fori_loop(first, last, body, tuple(q0) + tuple(q1) + tuple(v1), unroll=2)
            v = new
        return v

    v = adjoint_steps(0, 4, inj)

    for copy in o_copies:
        copy.wait()
    weighted = obs[mine] * weight_row
    squares = jnp.zeros((1, slots), F32)
    msend[:, 0] = jnp.zeros((nf, 8, LANES), F32)
    for q in range(npr):
        seen = obs[q]
        squares = squares + jnp.sum(seen * seen, axis=0, keepdims=True)
        tile = lax.dot_general(
            weighted, seen, (((1,), (1,)), ((), ())), precision=HIGHEST, preferred_element_type=F32
        )
        for f in range(nf):
            msend[f, 0, :, q * 8 : q * 8 + 8] = tile
    owner_iota = lax.broadcasted_iota(jnp.int32, (nf, slots), 0).astype(F32)
    owner_squares = jnp.where(owner_iota == owner_row, squares, 0.0)
    by_owner = jnp.dot(
        owner_squares,
        jnp.where(pos_hot, 1.0, 0.0),
        precision=HIGHEST,
        preferred_element_type=F32,
    )
    for o in range(nf):
        msend[o, 1] = jnp.broadcast_to(by_owner[o : o + 1, :], (8, LANES))
    mrecv[me] = msend[me]
    m_copies = []
    for j in range(1, nf):
        other = lax.rem(me + j, nf)
        copy = send(
            msend.at[other], mrecv.at[me], m_send.at[j - 1], m_recv.at[j - 1], {"field": other}
        )
        copy.start()
        m_copies.append(copy)

    v = adjoint_steps(4, STEPS, v)
    free = spare if v is state else state
    prior(v, HALO, end, ((None, 0), (free, 0), (inj, 0), (free, 0), (h_out, HALO)))

    for copy in m_copies:
        copy.wait()
    total = mrecv[0, 0]
    for f in range(1, nf):
        total = total + mrecv[f, 0]
    t_out[...] = total[:, : npr * 8] * (1.0 / math.sqrt(SENS_DEV * nf))
    for f in range(nf):
        sq2d[f : f + 1, :] = mrecv[f, 1][0:1, :]
    gate = jax.nn.sigmoid(logit[...])
    g_out[...] = gate * (1.0 - gate) * noise[...] * sq2d[:, :cap]


def on_device(
    probes,
    matern_shift,
    diffusivity,
    sensor_count,
    sensor_cell,
    sensor_owner,
    design_logit,
    noise_precision,
):
    nf, npr = lax.axis_size("field"), lax.axis_size("probe")
    count, nz, cx, ny = probes.shape
    cap, slots = design_logit.shape[2], sensor_cell.shape[1]
    halves = ny // LANES
    per = nz * halves
    wide = cx + 2 * HALO
    tiles_in = (
        probes.reshape(count, nz, cx, halves, LANES)
        .transpose(2, 1, 3, 0, 4)
        .reshape(cx * per, count, LANES)
    )
    coef_in = jnp.concatenate([diffusivity, matern_shift], axis=0).transpose(1, 0, 2)
    dims = (nf, npr, nz, cx, ny, cap, slots)
    vmem = pl.BlockSpec(memory_space=pltpu.VMEM)
    smem = pl.BlockSpec(memory_space=pltpu.SMEM)
    anywhere = pl.BlockSpec(memory_space=pl.ANY)
    dma = pltpu.SemaphoreType.DMA
    tall = pltpu.VMEM((wide * per, count, LANES), F32)
    hess, tiles, grad = pl.pallas_call(
        functools.partial(kernel, dims),
        out_shape=(
            jax.ShapeDtypeStruct((cx * per, count, LANES), F32),
            jax.ShapeDtypeStruct((count, npr * count), F32),
            jax.ShapeDtypeStruct((nf, cap), F32),
        ),
        in_specs=[anywhere, anywhere, smem, smem, vmem, vmem, vmem, vmem],
        out_specs=(vmem, vmem, vmem),
        scratch_shapes=[
            pltpu.VMEM((wide * per, count, LANES), jnp.bfloat16),
            pltpu.VMEM((wide, 2 * nz, ny), F32),
            tall,
            tall,
            tall,
            tall,
            tall,
            pltpu.VMEM((nf, LANES), F32),
            pltpu.VMEM((nf, 8, LANES), F32),
            pltpu.VMEM((nf, 8, LANES), F32),
            pltpu.VMEM((cx * nz, ny), F32),
            pltpu.VMEM((npr, count, slots), F32),
            pltpu.VMEM((nf, 2, 8, LANES), F32),
            pltpu.VMEM((nf, 2, 8, LANES), F32),
            pltpu.VMEM((nf, LANES), F32),
            dma((2,)),
            dma((6,)),
            dma((6,)),
            dma((nf - 1,)),
            dma((nf - 1,)),
            dma((npr - 1,)),
            dma((npr - 1,)),
            dma((nf - 1,)),
            dma((nf - 1,)),
        ],
        compiler_params=pltpu.CompilerParams(collective_id=0, has_side_effects=True),
        name="hessian_pass",
    )(
        tiles_in,
        coef_in,
        sensor_cell,
        sensor_count,
        sensor_cell,
        sensor_owner[:, :, 0],
        design_logit[0],
        noise_precision[0],
    )
    hess = (
        hess.reshape(cx, nz, halves, count, LANES)
        .transpose(3, 1, 0, 2, 4)
        .reshape(count, nz, cx, ny)
    )
    return hess, tiles, grad[None]


def solution(mesh):
    in_specs = (
        P("probe", None, "field", None),
        P(None, "field", None),
        P(None, "field", None),
        P("field"),
        P("field", None),
        P("field", None, None),
        P("field", None, None),
        P("field", None, None),
    )
    out_specs = (P("probe", None, "field", None), P("probe", None), P("field", None, None))
    return jax.shard_map(
        on_device, mesh=mesh, in_specs=in_specs, out_specs=out_specs, check_vma=False
    )
```

time: 236 us -> 79.3 us (0.34); the launches traced: 231 us -> 79 us
  starting transfers between devices: 78.5 us -> 0 us
  Pallas kernels: 0 us -> 69.4 us
  blocking collectives: 43.1 us -> 0 us
  other arithmetic: 31.7 us -> 0.75 us
  waiting for transfers between devices: 29.6 us -> 0 us
  local copies, waits for them, and re-layouts: 29.5 us -> 7.56 us
  between operations: 15.3 us -> 1.34 us
  matrix products: 3.61 us -> 0 us
    pallas_call x0 -> x1, Pallas kernels: none -> 69.4 us  [on_device(): pl.pallas_call(functools.partial(kernel, dims), out_shape=(jax.ShapeDtype...]
    ppermute x30 -> x0, starting transfers between devices: 67.2 us -> none  [the longest x15 61.2 us: with_halo(): after = lax.ppermute(first, axis, down)]
    psum x2 -> x0, blocking collectives: 34.1 us -> none  [the longest x1 29.7 us: on_device(): tiles = lax.psum(columns, 'field') * scale_factor]
    ppermute x30 -> x0, waiting for transfers between devices: 12.9 us -> none  [the longest x15 6.65 us: with_halo(): before = lax.ppermute(last, axis, up)]
    all_to_all x1 -> x0, starting transfers between devices: 11.3 us -> none  [on_device(): lax.all_to_all(outgoing, 'field', split_axis=0, concat_axis=0, tiled=True)]
    all_gather x1 -> x0, waiting for transfers between devices: 10.8 us -> none  [on_device(): piece = lax.all_gather(probes, 'probe', axis=0, tiled=True)]
    all_to_all x1 -> x0, blocking collectives: 9.07 us -> none  [on_device(): lax.all_to_all(weighted, 'field', split_axis=0, concat_axis=0, tiled=True)]
    sub x1 -> x0, local copies, waits for them, and re-layouts: 8.58 us -> none  [on_device(): middle + coef_mid * (beside_all - 6.0 * middle)]
  transfers between devices with their start and end apart: 32 -> 0, of which waited for: 25 -> 0; matrix products, arithmetic and copies ran while one was open for 3% -> 0% of each run, Pallas kernels for 0% -> 0%
where the time goes in v1:
time: 79.3 us; the launch traced here: 79 us
  Pallas kernels  69.4 us (88%)
  local copies, waits for them, and re-layouts  7.56 us (10%)
  between operations  1.34 us (2%)
    pallas_call x1, Pallas kernels, on_device(): pl.pallas_call(functools.partial(kernel, dims), out_shape=(jax.ShapeDtype...  69.4 us
    unnamed x12, local copies, waits for them, and re-layouts  2.45 us
    reshape x1, local copies, waits for them, and re-layouts, on_device(): hess = hess.reshape(cx, nz, halves, count, LANES).transpose(3, 1, 0, 2, 4...  1.81 us
    transpose x1, local copies, waits for them, and re-layouts, on_device(): hess = hess.reshape(cx, nz, halves, count, LANES).transpose(3, 1, 0, 2, 4...  1.77 us

profile of v1, /device:TPU:1, one launch (start us, length us, event | category | flops | bytes accessed | tf_op | source)
XLA Modules:
  0.0 79.0 jit_solution(5939235641714557279)
XLA Ops:
  1.3 0.0 copy-start.1
  1.3 0.0 copy-start
  1.3 1.1 %copy.13 = f32[4,32,256]{2,0,1:T(4,128)S(1)} copy(f32[4,32,256]{2,1,0:T(8,128)} %param.9) | data formatting | bytes 262144 | tf_op args[1]
  2.4 0.0 copy-done.1
  2.4 0.1 copy.12
  2.5 0.8 maximum_bitcast_fusion.c_in
  3.2 0.0 copy-done
  3.2 0.1 reshape.18
  3.3 1.4 %copy.11 = bf16[8,4,32,2,128]{4,0,3,1,2:T(8,128)(2,1)} copy(bf16[8,4,32,2,128]{4,3,2,1,0:T(2,128)(2,1)S(1)} %reshape.18) | data formatting | bytes 1048576 | tf_op jit(solution)/shard_map/reshape | solution.py:438
  4.8 69.4 %hessian_pass.1 = (f32[256,8,128]{2,1,0:T(8,128)}, f32[8,16]{1,0:T(8,128)}, f32[16,24]{1,0:T(8,128)}) custom-call(bf16[256,8,128]{2,1,0:T(8,128)(2,1)} %bitcast.14, f32[32,8,256]{2,1,0:T(8,128)} %maximum_bitcast_fusion.c_in, s32[1,256]{1,0:T(1,128)} %cell_v.1, s32[1]{0:T(128)S(6)} %copy.17.count_s, s32[1,256]{1,0:T(1,128)} %cell_v.1, s32[1,256]{1,0:T(1,128)} %bitcast.19, ...), custom_call_target="tpu_custom_call" | custom-call | tf_op jit(solution)/shard_map/hessian_pass/pallas_call | solution.py:449
  74.1 1.8 %copy.14 = f32[8,4,32,2,128]{4,3,2,1,0:T(2,128)S(1)} copy(f32[8,4,32,2,128]{4,0,3,1,2:T(8,128)} %bitcast.15) | data formatting | bytes 2097152 | tf_op jit(solution)/shard_map/transpose | solution.py:498
  75.9 0.0 copy-start.3
  75.9 1.8 %reshape.21 = f32[8,4,32,256]{3,2,1,0:T(8,128)} reshape(f32[8,4,32,2,128]{4,3,2,1,0:T(2,128)S(1)} %copy.14) | data formatting | bytes 2097152 | tf_op jit(solution)/shard_map/reshape | solution.py:499
  77.7 0.0 copy-done.3
  77.7 0.0 copy-start.2
  77.7 0.6 copy.18
  78.3 0.1 copy-done.2
  78.4 0.6 copy.19
Async XLA Ops:
  1.3 1.1 %copy-start.1 = (f32[4,32,256]{2,1,0:T(8,128)S(1)}, f32[4,32,256]{2,1,0:T(8,128)}, u32[]{:S(2)}) copy-start(f32[4,32,256]{2,1,0:T(8,128)} %param.10) | copy-start | bytes 393220
  1.3 1.9 %copy-start = (bf16[8,4,32,256]{3,2,1,0:T(8,128)(2,1)S(1)}, bf16[8,4,32,256]{3,2,1,0:T(8,128)(2,1)}, u32[]{:S(2)}) copy-start(bf16[8,4,32,256]{3,2,1,0:T(8,128)(2,1)} %param.8) | copy-start | bytes 1572868
  75.9 1.8 %copy-start.3 = (f32[8,16]{1,0:T(8,128)S(1)}, f32[8,16]{1,0:T(8,128)}, u32[]{:S(2)}) copy-start(f32[8,16]{1,0:T(8,128)} %get-tuple-element.13) | copy-start | bytes 1540
  77.7 0.7 copy-start.2

commit v2 on v1

--- a/solution.py
+++ b/solution.py
@@ -28,24 +28,33 @@
         ref[row * per + i] = values[i]
 
 
-def around(west, mid, east, halves, at_first, at_last):
+def around(west, mid, east, at_first, at_last):
     per = len(mid)
-    zero = jnp.zeros_like(mid[0])
-    fwd = [pltpu.roll(t, 1, 1) for t in mid]
-    bwd = [pltpu.roll(t, LANES - 1, 1) for t in mid]
     out = []
     for i in range(per):
-        half = i % halves
-        prev = fwd[i - 1] if half > 0 else zero
-        following = bwd[i + 1] if half < halves - 1 else zero
-        side = jnp.where(at_first, prev, fwd[i]) + jnp.where(at_last, following, bwd[i])
-        total = (west[i] + east[i]) + side
-        depth = [mid[j] for j in (i - halves, i + halves) if 0 <= j < per]
+        other = mid[i ^ 1]
+        if i % 2 == 0:
+            far = jnp.where(at_first, 0.0, pltpu.roll(other, 1, 1))
+        else:
+            far = jnp.where(at_last, 0.0, pltpu.roll(other, LANES - 1, 1))
+        total = (west[i] + east[i]) + (other + far)
+        depth = [mid[j] for j in (i - 2, i + 2) if 0 <= j < per]
         if len(depth) == 2:
             total = total + (depth[0] + depth[1])
         elif depth:
             total = total + depth[0]
         out.append(total)
+    return out
+
+
+def reorder(value, matrix):
+    out = None
+    for piece in range(3):
+        part = value.astype(jnp.bfloat16)
+        term = jnp.dot(part, matrix, preferred_element_type=F32)
+        out = term if out is None else out + term
+        if piece < 2:
+            value = value - part.astype(F32)
     return out
 
 
@@ -62,9 +71,11 @@
     h_out,
     t_out,
     g_out,
+    raw,
     src,
     coef,
     kap,
+    keep,
     rec,
     buf_a,
     buf_b,
@@ -97,7 +108,7 @@
     left = lax.rem(me + nf - 1, nf)
     right = lax.rem(me + 1, nf)
 
-    own_p = pltpu.make_async_copy(p_in, src.at[pl.ds(HALO * per, cx * per)], local_sem.at[0])
+    own_p = pltpu.make_async_copy(p_in, raw.at[pl.ds(HALO * nz, cx * nz)], local_sem.at[0])
     own_c = pltpu.make_async_copy(c_in, coef.at[pl.ds(HALO, cx)], local_sem.at[1])
     own_p.start()
     own_c.start()
@@ -149,7 +160,7 @@
         return [to_right, to_left]
 
     edge_c = halo_pair(c_in, 0, coef, 1, 0)
-    edge_p = halo_pair(p_in, 0, src, per, 2)
+    edge_p = halo_pair(p_in, 0, raw, nz, 2)
 
     gated = jax.nn.sigmoid(logit[...])
     wpad[...] = jnp.zeros_like(wpad)
@@ -178,7 +189,8 @@
     shift_z = shift_x + cx.bit_length() - 1
     line_row = ((cell >> shift_x) & (cx - 1)) * nz + (cell >> shift_z)
     owner_row = owner_v[...].astype(F32)
-    y_col = column((cell & (ny - 1)).astype(F32))
+    y_at = cell & (ny - 1)
+    y_col = column(((y_at & 1) * LANES + (y_at >> 1)).astype(F32))
     owner_col = column(owner_row)
     pos_col = jnp.sum(
         jnp.where(jnp.logical_and(owner_col == owner_row, lan < sub), 1.0, 0.0),
@@ -189,30 +201,55 @@
     lane_pos = lax.broadcasted_iota(jnp.int32, (slots, LANES), 1).astype(F32)
     pos_hot = lane_pos == pos_col
 
-    own_c.wait()
-    own_p.wait()
+    ny_sub = lax.broadcasted_iota(jnp.int32, (ny, ny), 0)
+    ny_lan = lax.broadcasted_iota(jnp.int32, (ny, ny), 1)
+    split = jnp.where(ny_sub == 2 * (ny_lan & (LANES - 1)) + (ny_lan >> 7), 1.0, 0.0)
+    split = split.astype(jnp.bfloat16)
+    merge = jnp.where(ny_lan == 2 * (ny_sub & (LANES - 1)) + (ny_sub >> 7), 1.0, 0.0)
+    merge = merge.astype(jnp.bfloat16)
+
+    def sort_coef(first, count_x):
+        value = coef[pl.ds(first, count_x)].reshape(count_x * 2 * nz, ny)
+        coef[pl.ds(first, count_x)] = reorder(value, split).reshape(count_x, 2 * nz, ny)
+
+    def sort_probes(first, count_x):
+        value = raw[pl.ds(first * nz, count_x * nz)].astype(F32)
+        value = value.reshape(count_x * nz * 8, ny).astype(jnp.bfloat16)
+        value = jnp.dot(value, split, preferred_element_type=F32)
+        for i in range(count_x * nz):
+            for h in range(halves):
+                src[(first * nz + i) * halves + h] = value[
+                    i * 8 : i * 8 + 8, h * LANES : (h + 1) * LANES
+                ]
 
     def spread(x, carry):
         tile = coef[x]
         for z in range(nz):
             for h in range(halves):
                 at = slice(h * LANES, (h + 1) * LANES)
-                kap[x * per + z * halves + h] = jnp.broadcast_to(tile[z : z + 1, at], (8, LANES))
-                rec[x * per + z * halves + h] = 1.0 / jnp.broadcast_to(
-                    tile[nz + z : nz + z + 1, at] + 6.0, (8, LANES)
-                )
+                row = x * per + z * halves + h
+                k = jnp.broadcast_to(tile[z : z + 1, at], (8, LANES))
+                kap[row] = k
+                keep[row] = (1.0 - ADVECT) - 6.0 * k
+                rec[row] = 1.0 / jnp.broadcast_to(tile[nz + z : nz + z + 1, at] + 6.0, (8, LANES))
         return carry
 
-    lax.fori_loop(HALO, end, spread, 0)
+    own_c.wait()
+    sort_coef(HALO, cx)
+    lax.fori_loop(HALO, end, spread, 0, unroll=2)
+    own_p.wait()
+    sort_probes(HALO, cx)
     for copy in edge_c:
         copy.wait()
-    lax.fori_loop(0, HALO, spread, 0)
-    lax.fori_loop(end, wide, spread, 0)
+    sort_coef(0, HALO)
+    sort_coef(end, HALO)
+    lax.fori_loop(0, HALO, spread, 0, unroll=2)
+    lax.fori_loop(end, wide, spread, 0, unroll=2)
 
     lane = lax.broadcasted_iota(jnp.int32, (8, LANES), 1)
     at_first = lane == 0
     at_last = lane == LANES - 1
-    ring = functools.partial(around, halves=halves, at_first=at_first, at_last=at_last)
+    ring = functools.partial(around, at_first=at_first, at_last=at_last)
     span = range(per)
 
     def prior(origin, out_first, out_last, buffers):
@@ -246,6 +283,8 @@
 
     for copy in edge_p:
         copy.wait()
+    sort_probes(0, HALO)
+    sort_probes(end, HALO)
     flip = ((None, 0), (buf_a, 0), (buf_b, 0), (buf_a, 0), (buf_b, 0))
     prior(src, HALO - STEPS, end + STEPS, flip)
 
@@ -254,31 +293,17 @@
         reach = STEPS - 1 - step
 
         def body(x, carry, u=u, new=new):
-            west, mid = carry[:per], carry[per:]
+            west = rows_of(u, x - 1, per)
+            mid = rows_of(u, x, per)
             east = rows_of(u, x + 1, per)
             ring_sum = ring(west, mid, east)
             k = rows_of(kap, x, per)
-            put_rows(
-                new,
-                x,
-                per,
-                [
-                    k[i] * ring_sum[i]
-                    + ((1.0 - ADVECT) - 6.0 * k[i]) * mid[i]
-                    + ADVECT * west[i]
-                    for i in span
-                ],
-            )
-            return tuple(mid) + tuple(east)
-
-        first, last = HALO - reach, end + reach
-        lax.fori_loop(
-            first,
-            last,
-            body,
-            tuple(rows_of(u, first - 1, per)) + tuple(rows_of(u, first, per)),
-            unroll=2,
-        )
+            c = rows_of(keep, x, per)
+            values = [k[i] * ring_sum[i] + (c[i] * mid[i] + ADVECT * west[i]) for i in span]
+            put_rows(new, x, per, values)
+            return carry
+
+        lax.fori_loop(HALO - reach, end + reach, body, 0, unroll=2)
     state = buf_b if STEPS % 2 == 0 else buf_a
     spare = buf_a if STEPS % 2 == 0 else buf_b
 
@@ -317,8 +342,8 @@
             c = cell_s[0, part * LANES + s]
             y = c & (ny - 1)
             at = (HALO + ((c >> shift_x) & (cx - 1))) * per
-            at = at + (c >> shift_z) * halves + (y >> 7)
-            turn = (s - y) & (LANES - 1)
+            at = at + (c >> shift_z) * halves + (y & 1)
+            turn = (s - (y >> 1)) & (LANES - 1)
             return jnp.where(lane == s, pltpu.roll(state[at], turn, 1), held)
 
         held = lax.fori_loop(0, LANES, pick, jnp.zeros((8, LANES), F32), unroll=8)
@@ -341,29 +366,23 @@
             new = spare if step % 2 == 0 else state
 
             def body(x, carry, v=v, new=new):
-                q_west, q_mid, mid = carry[:per], carry[per : 2 * per], carry[2 * per :]
+                q_west, q_mid = carry[:per], carry[per:]
+                mid = rows_of(v, x, per)
                 east = rows_of(v, x + 1, per)
                 k = rows_of(kap, x + 1, per)
+                c = rows_of(keep, x, per)
                 q_east = [k[i] * east[i] for i in span]
                 ring_sum = ring(q_west, q_mid, q_east)
-                put_rows(
-                    new,
-                    x,
-                    per,
-                    [
-                        (ring_sum[i] - 6.0 * q_mid[i])
-                        + ((1.0 - ADVECT) * mid[i] + ADVECT * east[i])
-                        for i in span
-                    ],
-                )
-                return tuple(q_mid) + tuple(q_east) + tuple(east)
+                values = [ring_sum[i] + (c[i] * mid[i] + ADVECT * east[i]) for i in span]
+                put_rows(new, x, per, values)
+                return tuple(q_mid) + tuple(q_east)
 
             first, last = step + 1, wide - step - 1
             v0, v1 = rows_of(v, first - 1, per), rows_of(v, first, per)
             k0, k1 = rows_of(kap, first - 1, per), rows_of(kap, first, per)
             q0 = [k0[i] * v0[i] for i in span]
             q1 = [k1[i] * v1[i] for i in span]
-            lax.fori_loop(first, last, body, tuple(q0) + tuple(q1) + tuple(v1), unroll=2)
+            lax.fori_loop(first, last, body, tuple(q0) + tuple(q1), unroll=2)
             v = new
         return v
 
@@ -404,7 +423,16 @@
 
     v = adjoint_steps(4, STEPS, v)
     free = spare if v is state else state
-    prior(v, HALO, end, ((None, 0), (free, 0), (inj, 0), (free, 0), (h_out, HALO)))
+    prior(v, HALO, end, ((None, 0), (free, 0), (inj, 0), (free, 0), (inj, 0)))
+
+    chunk = cx // 4
+    for first in range(0, cx, chunk):
+        tiles = inj[pl.ds((HALO + first) * per, chunk * per)]
+        tiles = tiles.reshape(chunk * nz, halves, 8, LANES)
+        sides = [tiles[:, h].reshape(chunk * nz * 8, LANES) for h in range(halves)]
+        value = reorder(jnp.concatenate(sides, axis=1), merge)
+        h_out[pl.ds(first * nz, chunk * nz)] = value.reshape(chunk * nz, 8, ny)
+
 
     for copy in m_copies:
         copy.wait()
@@ -434,11 +462,7 @@
     halves = ny // LANES
     per = nz * halves
     wide = cx + 2 * HALO
-    tiles_in = (
-        probes.reshape(count, nz, cx, halves, LANES)
-        .transpose(2, 1, 3, 0, 4)
-        .reshape(cx * per, count, LANES)
-    )
+    tiles_in = probes.transpose(2, 1, 0, 3).reshape(cx * nz, count, ny)
     coef_in = jnp.concatenate([diffusivity, matern_shift], axis=0).transpose(1, 0, 2)
     dims = (nf, npr, nz, cx, ny, cap, slots)
     vmem = pl.BlockSpec(memory_space=pltpu.VMEM)
@@ -449,15 +473,17 @@
     hess, tiles, grad = pl.pallas_call(
         functools.partial(kernel, dims),
         out_shape=(
-            jax.ShapeDtypeStruct((cx * per, count, LANES), F32),
+            jax.ShapeDtypeStruct((cx * nz, count, ny), F32),
             jax.ShapeDtypeStruct((count, npr * count), F32),
             jax.ShapeDtypeStruct((nf, cap), F32),
         ),
         in_specs=[anywhere, anywhere, smem, smem, vmem, vmem, vmem, vmem],
         out_specs=(vmem, vmem, vmem),
         scratch_shapes=[
-            pltpu.VMEM((wide * per, count, LANES), jnp.bfloat16),
+            pltpu.VMEM((wide * nz, count, ny), jnp.bfloat16),
+            tall,
             pltpu.VMEM((wide, 2 * nz, ny), F32),
+            tall,
             tall,
             tall,
             tall,
@@ -493,11 +519,7 @@
         design_logit[0],
         noise_precision[0],
     )
-    hess = (
-        hess.reshape(cx, nz, halves, count, LANES)
-        .transpose(3, 1, 0, 2, 4)
-        .reshape(count, nz, cx, ny)
-    )
+    hess = hess.reshape(cx, nz, count, ny).transpose(2, 1, 0, 3)
     return hess, tiles, grad[None]
 
 

time: 79.3 us -> 71.8 us (0.905)
  Pallas kernels: 69.4 us -> 63.1 us
  local copies, waits for them, and re-layouts: 7.56 us -> 6.34 us
    pallas_call x1, Pallas kernels: 69.4 us -> 63.1 us  [on_device(): pl.pallas_call(functools.partial(kernel, dims), out_shape=(jax.ShapeDtype...]
    reshape x3 -> x1, local copies, waits for them, and re-layouts: 3.34 us -> 2.81 us  [on_device(): hess = hess.reshape(cx, nz, count, ny).transpose(2, 1, 0, 3)]
where the time goes in v2:
time: 71.8 us; the launch traced here: 71.6 us
  Pallas kernels  63.1 us (88%)
  local copies, waits for them, and re-layouts  6.34 us (9%)
  between operations  1.33 us (2%)
  other arithmetic  0.75 us (1%)
    pallas_call x1, Pallas kernels, on_device(): pl.pallas_call(functools.partial(kernel, dims), out_shape=(jax.ShapeDtype...  63.1 us
    reshape x1, local copies, waits for them, and re-layouts, on_device(): hess = hess.reshape(cx, nz, count, ny).transpose(2, 1, 0, 3)  2.81 us
    unnamed x12, local copies, waits for them, and re-layouts  2.45 us

profile of v2, /device:TPU:1, one launch (start us, length us, event | category | flops | bytes accessed | tf_op | source)
XLA Modules:
  0.0 71.6 jit_solution(7231349294157010427)
XLA Ops:
  1.3 0.0 copy-start.1
  1.3 0.0 copy-start
  1.3 1.1 %copy.13 = f32[4,32,256]{2,0,1:T(4,128)S(1)} copy(f32[4,32,256]{2,1,0:T(8,128)} %param.9) | data formatting | bytes 262144 | tf_op args[1]
  2.4 0.0 copy-done.1
  2.4 0.1 copy.12
  2.5 0.8 %maximum_bitcast_fusion.c_in = f32[32,8,256]{2,1,0:T(8,128)} fusion(f32[4,32,256]{2,0,1:T(4,128)S(1)} %copy.13, f32[4,32,256]{2,0,1:T(4,128)S(1)} %copy.12), kind=kLoop, calls=%fused_computation.1 | loop fusion | flops 65536 | bytes 524288 | tf_op jit(solution)/shard_map/transpose | solution.py:466
  3.2 0.0 copy-done
  3.2 1.1 %copy.11 = bf16[32,4,8,256]{3,2,1,0:T(8,128)(2,1)} copy(bf16[32,4,8,256]{3,0,1,2:T(8,128)(2,1)S(1)} %bitcast.15) | data formatting | bytes 1048576 | tf_op jit(solution)/shard_map/transpose | solution.py:465
  4.3 63.1 %hessian_pass.1 = (f32[128,8,256]{2,1,0:T(8,128)}, f32[8,16]{1,0:T(8,128)}, f32[16,24]{1,0:T(8,128)}) custom-call(bf16[128,8,256]{2,1,0:T(8,128)(2,1)} %bitcast.12, f32[32,8,256]{2,1,0:T(8,128)} %maximum_bitcast_fusion.c_in, s32[1,256]{1,0:T(1,128)} %cell_v.1, s32[1]{0:T(128)S(6)} %copy.19.count_s, s32[1,256]{1,0:T(1,128)} %cell_v.1, s32[1,256]{1,0:T(1,128)} %bitcast.19, ...), custom_call_target="tpu_custom_call" | custom-call | tf_op jit(solution)/shard_map/hessian_pass/pallas_call | solution.py:473
  67.4 0.0 copy-start.3
  67.4 2.8 %copy.16 = f32[32,4,8,256]{3,0,1,2:T(8,128)} copy(f32[32,4,8,256]{3,2,1,0:T(8,128)} %bitcast.14) | data formatting | bytes 2097152 | tf_op jit(solution)/shard_map/reshape | solution.py:522
  70.3 0.0 copy-start.2
  70.3 0.0 copy-done.3
  70.3 0.6 copy.20
  70.9 0.1 copy-done.2
  71.0 0.6 copy.21
Async XLA Ops:
  1.3 1.1 %copy-start.1 = (f32[4,32,256]{2,1,0:T(8,128)S(1)}, f32[4,32,256]{2,1,0:T(8,128)}, u32[]{:S(2)}) copy-start(f32[4,32,256]{2,1,0:T(8,128)} %param.10) | copy-start | bytes 393220
  1.3 1.9 %copy-start = (bf16[8,4,32,256]{3,2,1,0:T(8,128)(2,1)S(1)}, bf16[8,4,32,256]{3,2,1,0:T(8,128)(2,1)}, u32[]{:S(2)}) copy-start(bf16[8,4,32,256]{3,2,1,0:T(8,128)(2,1)} %param.8) | copy-start | bytes 1572868
  67.4 2.8 %copy-start.3 = (f32[8,16]{1,0:T(8,128)S(1)}, f32[8,16]{1,0:T(8,128)}, u32[]{:S(2)}) copy-start(f32[8,16]{1,0:T(8,128)} %get-tuple-element.13) | copy-start | bytes 1540
  70.3 0.7 copy-start.2
